TPU v7x, 256 devices: a whole 4x4x8 slice. The times are simulated.
256 devices in a mesh: prow: 32 (over y, z), pcol: 8 (over x, core).
Axes of the slice: x: 4, y: 4, z: 8, core: 2. Of those that a mesh axis runs over, the one named last changes fastest.
Arguments:
- right_side: bfloat16 [32, 6, 128, 256], P('prow'), may hold values from -6 to 6
- lower_inverse: bfloat16 [32, 6, 256, 256], P('prow'), as said below
- upper_inverse: bfloat16 [32, 6, 256, 256], P('prow'), as said below
- lower_blocks: bfloat16 [32, 5, 48, 256, 256], P('prow', None, 'pcol'), may hold values from -0.0546875 to 0.0546875
- lower_sources: int32 [32, 5, 48], P('prow', None, 'pcol'), may hold values from 0 to 159, as said below
- lower_counts: int32 [32, 5, 8], P('prow', None, 'pcol'), may hold values from 1 to 6, as said below
- upper_blocks: bfloat16 [32, 5, 48, 256, 256], P('prow', None, 'pcol'), may hold values from -0.0546875 to 0.0546875
- upper_sources: int32 [32, 5, 48], P('prow', None, 'pcol'), may hold values from 32 to 191, as said below
- upper_counts: int32 [32, 5, 8], P('prow', None, 'pcol'), may hold values from 1 to 6, as said below
Outputs:
- solution: bfloat16 [32, 6, 128, 256], P('prow')
Inputs may be any that keep to these rules, and one draw needn't show every extreme that they name: `lower_sources`: entry [r, l, c] names supernode v * 32 + p of a level v below l + 1, with p % (8) == c // 6; entries may repeat. `upper_sources`: entry [r, l, c] names supernode v * 32 + p of a level v above l, with p % (8) == c // 6; entries may repeat. `lower_counts`: entry [r, l, g] is how many of the 6 slots of group g are live; the live ones come first. `upper_counts`: entry [r, l, g] is how many of the 6 slots of group g are live; the live ones come first. `lower_inverse`: each block is lower triangular. `upper_inverse`: each block is upper triangular.
All inputs are finite; a program needn't handle non-finite values.
Results may differ from a plain program's by a relative error of at most 0.02.
Values may be sent and summed in bfloat16 or wider, within the bound.
No kernel may reach another device: no remote copies, remote signals or barrier semaphores. Data moves between devices by JAX's collectives and lax.ppermute only.
A program may use at most 64 MiB of HBM per device.

v0:
```python
import jax
import jax.numpy as jnp
from jax import lax
from jax.sharding import PartitionSpec as P


def pick_sources(sources, count, store, width, ncol):
    group = store.shape[1]
    flat = store.reshape(store.shape[0] * group, store.shape[2], store.shape[3])
    position = sources // width * group + sources % width // ncol
    picked = flat[position]
    live = jnp.arange(sources.shape[0], dtype=jnp.int32) < count
    return jnp.where(live[:, None, None], picked, jnp.zeros_like(picked))


def contract(picked, blocks):
    return lax.dot_general(
        picked, blocks, (((0, 2), (0, 2)), ((), ())), preferred_element_type=jnp.float32
    )


def apply_inverse(residual, inverse):
    product = lax.dot_general(
        residual, inverse, (((1,), (1,)), ((), ())), preferred_element_type=jnp.float32
    )
    return product.astype(jnp.bfloat16)


def solve_level(right, inverse, blocks, sources, count, store):
    width = lax.axis_size("prow")
    ncol = lax.axis_size("pcol")
    picked = pick_sources(sources, count, store, width, ncol)
    total = lax.psum(contract(picked, blocks), "pcol")
    residual = (right.astype(jnp.float32) - total).astype(jnp.bfloat16)
    return apply_inverse(residual, inverse)


def spread(solved):
    ncol = lax.axis_size("pcol")
    column = lax.axis_index("pcol")
    whole = lax.all_gather(solved[None], "prow", axis=0, tiled=True)
    whole = whole.reshape(whole.shape[0] // ncol, ncol, whole.shape[1], whole.shape[2])
    return lax.dynamic_index_in_dim(whole, column, 1, keepdims=False)


def shards(
    right_side,
    lower_inverse,
    upper_inverse,
    lower_blocks,
    lower_sources,
    lower_counts,
    upper_blocks,
    upper_sources,
    upper_counts,
):
    group = lax.axis_size("prow") // lax.axis_size("pcol")
    levels = right_side.shape[1]
    shape = (levels, group, right_side.shape[2], right_side.shape[3])
    forward_store = jnp.zeros(shape, jnp.bfloat16)
    forward_own = []
    for level in range(levels):
        if level == 0:
            solved = apply_inverse(right_side[0, 0], lower_inverse[0, 0])
        else:
            solved = solve_level(
                right_side[0, level],
                lower_inverse[0, level],
                lower_blocks[0, level - 1],
                lower_sources[0, level - 1],
                lower_counts[0, level - 1, 0],
                forward_store,
            )
        forward_own.append(solved)
        if level + 1 < levels:
            forward_store = forward_store.at[level].set(spread(solved))
    backward_store = jnp.zeros(shape, jnp.bfloat16)
    backward_own = [None] * levels
    for level in range(levels - 1, -1, -1):
        if level == levels - 1:
            solved = apply_inverse(forward_own[level], upper_inverse[0, level])
        else:
            solved = solve_level(
                forward_own[level],
                upper_inverse[0, level],
                upper_blocks[0, level],
                upper_sources[0, level],
                upper_counts[0, level, 0],
                backward_store,
            )
        backward_own[level] = solved
        if level > 0:
            backward_store = backward_store.at[level].set(spread(solved))
    return jnp.stack(backward_own)[None]


def solution(mesh):
    in_specs = (
        P("prow", None, None, None),
        P("prow", None, None, None),
        P("prow", None, None, None),
        P("prow", None, "pcol", None, None),
        P("prow", None, "pcol"),
        P("prow", None, "pcol"),
        P("prow", None, "pcol", None, None),
        P("prow", None, "pcol"),
        P("prow", None, "pcol"),
    )
    out_specs = P("prow", None, None, None)
    return jax.shard_map(shards, mesh=mesh, in_specs=in_specs, out_specs=out_specs, check_vma=False)
```

profile of v0, /device:TPU:8, one launch (start us, length us, event | category | flops | bytes accessed | tf_op | source)
XLA Modules:
  0.0 1472.5 jit_solution(6980355928719453003)
XLA Ops:
  6.5 1.8 convolution_convert_fusion.11
  12.0 77.6 %all-gather.21.cloned.1.call-done = bf16[4096,256]{1,0:T(8,128)(2,1)} async-done(((bf16[128,256]{1,0:T(8,128)(2,1)}), bf16[4096,256]{1,0:T(8,128)(2,1)}) %all-gather.21.cloned.1.call-update) | async-done | bytes 2097168 | tf_op jit(solution)/shard_map/all_gather | solution.py:41
  91.3 2.2 convolution_bitcast_fusion.9
  93.6 62.8 %all-reduce.13.cloned.1.call-done = f32[128,256]{1,0:T(8,128)} async-done(((f32[128,256]{1,0:T(8,128)}), f32[128,256]{1,0:T(8,128)}) %all-reduce.13.cloned.1.call-update) | async-done | bytes 131088 | tf_op jit(solution)/shard_map/psum | solution.py:33
  159.0 76.3 %all-gather.23.cloned.1.call-done = bf16[4096,256]{1,0:T(8,128)(2,1)} async-done(((bf16[128,256]{1,0:T(8,128)(2,1)}), bf16[4096,256]{1,0:T(8,128)(2,1)}) %all-gather.23.cloned.1.call-update) | async-done | bytes 2097168 | tf_op jit(solution)/shard_map/all_gather | solution.py:41
  236.8 2.2 convolution_bitcast_fusion.8
  239.1 62.8 %all-reduce.15.cloned.1.call-done = f32[128,256]{1,0:T(8,128)} async-done(((f32[128,256]{1,0:T(8,128)}), f32[128,256]{1,0:T(8,128)}) %all-reduce.15.cloned.1.call-update) | async-done | bytes 131088 | tf_op jit(solution)/shard_map/psum | solution.py:33
  304.4 75.8 %all-gather.25.cloned.1.call-done = bf16[4096,256]{1,0:T(8,128)(2,1)} async-done(((bf16[128,256]{1,0:T(8,128)(2,1)}), bf16[4096,256]{1,0:T(8,128)(2,1)}) %all-gather.25.cloned.1.call-update) | async-done | bytes 2097168 | tf_op jit(solution)/shard_map/all_gather | solution.py:41
  381.7 2.2 convolution_bitcast_fusion.7
  384.0 62.8 %all-reduce.17.cloned.1.call-done = f32[128,256]{1,0:T(8,128)} async-done(((f32[128,256]{1,0:T(8,128)}), f32[128,256]{1,0:T(8,128)}) %all-reduce.17.cloned.1.call-update) | async-done | bytes 131088 | tf_op jit(solution)/shard_map/psum | solution.py:33
  449.3 76.3 %all-gather.27.cloned.1.call-done = bf16[4096,256]{1,0:T(8,128)(2,1)} async-done(((bf16[128,256]{1,0:T(8,128)(2,1)}), bf16[4096,256]{1,0:T(8,128)(2,1)}) %all-gather.27.cloned.1.call-update) | async-done | bytes 2097168 | tf_op jit(solution)/shard_map/all_gather | solution.py:41
  527.2 2.2 convolution_bitcast_fusion.6
  529.4 62.8 %all-reduce.19.cloned.1.call-done = f32[128,256]{1,0:T(8,128)} async-done(((f32[128,256]{1,0:T(8,128)}), f32[128,256]{1,0:T(8,128)}) %all-reduce.19.cloned.1.call-update) | async-done | bytes 131088 | tf_op jit(solution)/shard_map/psum | solution.py:33
  595.8 74.9 %all-gather.29.cloned.1.call-done = bf16[4096,256]{1,0:T(8,128)(2,1)} async-done(((bf16[128,256]{1,0:T(8,128)(2,1)}), bf16[4096,256]{1,0:T(8,128)(2,1)}) %all-gather.29.cloned.1.call-update) | async-done | bytes 2097168 | tf_op jit(solution)/shard_map/all_gather | solution.py:41
  672.3 2.2 convolution_bitcast_fusion.5
  674.5 62.8 %all-reduce.21.cloned.1.call-done = f32[128,256]{1,0:T(8,128)} async-done(((f32[128,256]{1,0:T(8,128)}), f32[128,256]{1,0:T(8,128)}) %all-reduce.21.cloned.1.call-update) | async-done | bytes 131088 | tf_op jit(solution)/shard_map/psum | solution.py:33
  737.4 1.9 convolution_convert_fusion.5
  741.3 74.9 %all-gather.31.cloned.1.call-done = bf16[4096,256]{1,0:T(8,128)(2,1)} async-done(((bf16[128,256]{1,0:T(8,128)(2,1)}), bf16[4096,256]{1,0:T(8,128)(2,1)}) %all-gather.31.cloned.1.call-update) | async-done | bytes 2097168 | tf_op jit(solution)/shard_map/all_gather | solution.py:41
  817.9 2.2 convolution_bitcast_fusion.4
  820.2 62.8 %all-reduce.23.cloned.1.call-done = f32[128,256]{1,0:T(8,128)} async-done(((f32[128,256]{1,0:T(8,128)}), f32[128,256]{1,0:T(8,128)}) %all-reduce.23.cloned.1.call-update) | async-done | bytes 131088 | tf_op jit(solution)/shard_map/psum | solution.py:33
  885.5 75.9 %all-gather.33.cloned.1.call-done = bf16[4096,256]{1,0:T(8,128)(2,1)} async-done(((bf16[128,256]{1,0:T(8,128)(2,1)}), bf16[4096,256]{1,0:T(8,128)(2,1)}) %all-gather.33.cloned.1.call-update) | async-done | bytes 2097168 | tf_op jit(solution)/shard_map/all_gather | solution.py:41
  963.0 2.2 convolution_bitcast_fusion.3
  965.3 62.8 %all-reduce.25.cloned.1.call-done = f32[128,256]{1,0:T(8,128)} async-done(((f32[128,256]{1,0:T(8,128)}), f32[128,256]{1,0:T(8,128)}) %all-reduce.25.cloned.1.call-update) | async-done | bytes 131088 | tf_op jit(solution)/shard_map/psum | solution.py:33
  1030.5 76.2 %all-gather.35.cloned.1.call-done = bf16[4096,256]{1,0:T(8,128)(2,1)} async-done(((bf16[128,256]{1,0:T(8,128)(2,1)}), bf16[4096,256]{1,0:T(8,128)(2,1)}) %all-gather.35.cloned.1.call-update) | async-done | bytes 2097168 | tf_op jit(solution)/shard_map/all_gather | solution.py:41
  1108.3 2.2 convolution_bitcast_fusion.2
  1110.6 62.8 %all-reduce.27.cloned.1.call-done = f32[128,256]{1,0:T(8,128)} async-done(((f32[128,256]{1,0:T(8,128)}), f32[128,256]{1,0:T(8,128)}) %all-reduce.27.cloned.1.call-update) | async-done | bytes 131088 | tf_op jit(solution)/shard_map/psum | solution.py:33
  1175.8 75.9 %all-gather.37.cloned.1.call-done = bf16[4096,256]{1,0:T(8,128)(2,1)} async-done(((bf16[128,256]{1,0:T(8,128)(2,1)}), bf16[4096,256]{1,0:T(8,128)(2,1)}) %all-gather.37.cloned.1.call-update) | async-done | bytes 2097168 | tf_op jit(solution)/shard_map/all_gather | solution.py:41
  1253.2 2.2 convolution_bitcast_fusion.1
  1255.5 62.8 %all-reduce.29.cloned.1.call-done = f32[128,256]{1,0:T(8,128)} async-done(((f32[128,256]{1,0:T(8,128)}), f32[128,256]{1,0:T(8,128)}) %all-reduce.29.cloned.1.call-update) | async-done | bytes 131088 | tf_op jit(solution)/shard_map/psum | solution.py:33
  1320.8 76.3 %all-gather.39.cloned.1.call-done = bf16[4096,256]{1,0:T(8,128)(2,1)} async-done(((bf16[128,256]{1,0:T(8,128)(2,1)}), bf16[4096,256]{1,0:T(8,128)(2,1)}) %all-gather.39.cloned.1.call-update) | async-done | bytes 2097168 | tf_op jit(solution)/shard_map/all_gather | solution.py:41
  1398.7 2.2 convolution_bitcast_fusion
  1400.9 62.8 %all-reduce.31.cloned.1.call-done = f32[128,256]{1,0:T(8,128)} async-done(((f32[128,256]{1,0:T(8,128)}), f32[128,256]{1,0:T(8,128)}) %all-reduce.31.cloned.1.call-update) | async-done | bytes 131088 | tf_op jit(solution)/shard_map/psum | solution.py:33
  (133 shorter events, 44.5 us)
Async XLA Ops:
  6.5 83.1 %all-gather.21.cloned.1.call-start = ((), (), s32[]{:S(2)}) async-start(), calls=%async_computation.10 | async-start | bytes 2162688 | tf_op jit(solution)/shard_map/all_gather | solution.py:41
  8.3 148.1 %all-reduce.13.cloned.1.call-start = ((), (), s32[]{:S(2)}) async-start(), calls=%async_computation | async-start | bytes 262144 | tf_op jit(solution)/shard_map/psum | solution.py:33
  93.6 141.7 %all-gather.23.cloned.1.call-start = ((), (), s32[]{:S(2)}) async-start(), calls=%async_computation.11 | async-start | bytes 2162688 | tf_op jit(solution)/shard_map/all_gather | solution.py:41
  158.2 143.7 %all-reduce.15.cloned.1.call-start = ((), (), s32[]{:S(2)}) async-start(), calls=%async_computation.1 | async-start | bytes 262144 | tf_op jit(solution)/shard_map/psum | solution.py:33
  239.0 141.2 %all-gather.25.cloned.1.call-start = ((), (), s32[]{:S(2)}) async-start(), calls=%async_computation.12 | async-start | bytes 2162688 | tf_op jit(solution)/shard_map/all_gather | solution.py:41
  303.6 143.2 %all-reduce.17.cloned.1.call-start = ((), (), s32[]{:S(2)}) async-start(), calls=%async_computation.2 | async-start | bytes 262144 | tf_op jit(solution)/shard_map/psum | solution.py:33
  383.9 141.7 %all-gather.27.cloned.1.call-start = ((), (), s32[]{:S(2)}) async-start(), calls=%async_computation.13 | async-start | bytes 2162688 | tf_op jit(solution)/shard_map/all_gather | solution.py:41
  448.6 143.7 %all-reduce.19.cloned.1.call-start = ((), (), s32[]{:S(2)}) async-start(), calls=%async_computation.3 | async-start | bytes 262144 | tf_op jit(solution)/shard_map/psum | solution.py:33
  529.3 208.0 %copy-start = (bf16[1,6,256,256]{3,2,1,0:T(8,128)(2,1)S(1)}, bf16[1,6,256,256]{3,2,1,0:T(8,128)(2,1)}, u32[]{:S(2)}) copy-start(bf16[1,6,256,256]{3,2,1,0:T(8,128)(2,1)} %param.31) | copy-start | bytes 2359300
  529.4 209.9 %copy-start.13 = (s32[1,5,1]{1,2,0:T(1,128)S(1)}, s32[1,5,1]{1,2,0:T(1,128)}, u32[]{:S(2)}) copy-start(s32[1,5,1]{1,2,0:T(1,128)} %param.37) | copy-start | bytes 64
  529.4 141.3 %all-gather.29.cloned.1.call-start = ((), (), s32[]{:S(2)}) async-start(), calls=%async_computation.14 | async-start | bytes 2162688 | tf_op jit(solution)/shard_map/all_gather | solution.py:41
  594.0 143.4 %all-reduce.21.cloned.1.call-start = ((), (), s32[]{:S(2)}) async-start(), calls=%async_computation.4 | async-start | bytes 262144 | tf_op jit(solution)/shard_map/psum | solution.py:33
  674.5 141.7 %all-gather.31.cloned.1.call-start = ((), (), s32[]{:S(2)}) async-start(), calls=%async_computation.15 | async-start | bytes 2162688 | tf_op jit(solution)/shard_map/all_gather | solution.py:41
  739.2 143.7 %all-reduce.23.cloned.1.call-start = ((), (), s32[]{:S(2)}) async-start(), calls=%async_computation.5 | async-start | bytes 262144 | tf_op jit(solution)/shard_map/psum | solution.py:33
  820.1 208.0 %copy-start.9 = (bf16[128,256]{1,0:T(8,128)(2,1)S(1)}, bf16[128,256]{1,0:T(8,128)(2,1)}, u32[]{:S(2)}) copy-start(bf16[128,256]{1,0:T(8,128)(2,1)} %convolution_convert_fusion.8) | copy-start | bytes 196612
  820.1 210.4 %copy-start.15 = (s32[6]{0:T(128)S(1)}, s32[6]{0:T(128)}, u32[]{:S(2)}) copy-start(s32[6]{0:T(128)} %get-tuple-element.148) | copy-start | bytes 76
  820.1 141.3 %all-gather.33.cloned.1.call-start = ((), (), s32[]{:S(2)}) async-start(), calls=%async_computation.16 | async-start | bytes 2162688 | tf_op jit(solution)/shard_map/all_gather | solution.py:41
  884.7 143.3 %all-reduce.25.cloned.1.call-start = ((), (), s32[]{:S(2)}) async-start(), calls=%async_computation.6 | async-start | bytes 262144 | tf_op jit(solution)/shard_map/psum | solution.py:33
  965.2 208.2 %copy-start.8 = (bf16[128,256]{1,0:T(8,128)(2,1)S(1)}, bf16[128,256]{1,0:T(8,128)(2,1)}, u32[]{:S(2)}) copy-start(bf16[128,256]{1,0:T(8,128)(2,1)} %convolution_convert_fusion.9) | copy-start | bytes 196612
  965.2 141.5 %all-gather.35.cloned.1.call-start = ((), (), s32[]{:S(2)}) async-start(), calls=%async_computation.17 | async-start | bytes 2162688 | tf_op jit(solution)/shard_map/all_gather | solution.py:41
  1029.8 143.5 %all-reduce.27.cloned.1.call-start = ((), (), s32[]{:S(2)}) async-start(), calls=%async_computation.7 | async-start | bytes 262144 | tf_op jit(solution)/shard_map/psum | solution.py:33
  1110.5 207.8 %copy-start.7 = (bf16[128,256]{1,0:T(8,128)(2,1)S(1)}, bf16[128,256]{1,0:T(8,128)(2,1)}, u32[]{:S(2)}) copy-start(bf16[128,256]{1,0:T(8,128)(2,1)} %convolution_convert_fusion.10) | copy-start | bytes 196612
  1110.5 141.2 %all-gather.37.cloned.1.call-start = ((), (), s32[]{:S(2)}) async-start(), calls=%async_computation.18 | async-start | bytes 2162688 | tf_op jit(solution)/shard_map/all_gather | solution.py:41
  1175.1 143.2 %all-reduce.29.cloned.1.call-start = ((), (), s32[]{:S(2)}) async-start(), calls=%async_computation.8 | async-start | bytes 262144 | tf_op jit(solution)/shard_map/psum | solution.py:33
  1255.4 208.3 %copy-start.6 = (bf16[128,256]{1,0:T(8,128)(2,1)S(1)}, bf16[128,256]{1,0:T(8,128)(2,1)}, u32[]{:S(2)}) copy-start(bf16[128,256]{1,0:T(8,128)(2,1)} %convolution_convert_fusion.11) | copy-start | bytes 196612
  1255.5 209.4 %copy-start.4 = (bf16[128,256]{1,0:T(8,128)(2,1)S(1)}, bf16[128,256]{1,0:T(8,128)(2,1)}, u32[]{:S(2)}) copy-start(bf16[128,256]{1,0:T(8,128)(2,1)} %convolution_convert_fusion.2) | copy-start | bytes 196612
  1255.5 209.4 %copy-start.3 = (bf16[128,256]{1,0:T(8,128)(2,1)S(1)}, bf16[128,256]{1,0:T(8,128)(2,1)}, u32[]{:S(2)}) copy-start(bf16[128,256]{1,0:T(8,128)(2,1)} %convolution_convert_fusion.3) | copy-start | bytes 196612
  1255.5 141.6 %all-gather.39.cloned.1.call-start = ((), (), s32[]{:S(2)}) async-start(), calls=%async_computation.19 | async-start | bytes 2162688 | tf_op jit(solution)/shard_map/all_gather | solution.py:41
  1320.1 144.8 %copy-start.5 = (bf16[128,256]{1,0:T(8,128)(2,1)S(1)}, bf16[128,256]{1,0:T(8,128)(2,1)}, u32[]{:S(2)}) copy-start(bf16[128,256]{1,0:T(8,128)(2,1)} %convolution_convert_fusion.1) | copy-start | bytes 196612
  1320.1 144.9 %copy-start.2 = (bf16[128,256]{1,0:T(8,128)(2,1)S(1)}, bf16[128,256]{1,0:T(8,128)(2,1)}, u32[]{:S(2)}) copy-start(bf16[128,256]{1,0:T(8,128)(2,1)} %convolution_convert_fusion.4) | copy-start | bytes 196612
  1320.1 144.9 %copy-start.11 = (bf16[128,256]{1,0:T(8,128)(2,1)S(1)}, bf16[128,256]{1,0:T(8,128)(2,1)}, u32[]{:S(2)}) copy-start(bf16[128,256]{1,0:T(8,128)(2,1)} %convolution_convert_fusion.5) | copy-start | bytes 196612
  1320.1 143.6 %all-reduce.31.cloned.1.call-start = ((), (), s32[]{:S(2)}) async-start(), calls=%async_computation.9 | async-start | bytes 262144 | tf_op jit(solution)/shard_map/psum | solution.py:33
  (5 other events, 266.6 us)
Sparse Core Ops, SparseCore 0:
  9.9 79.6 all-gather.20
  93.7 62.6 all-reduce.12
  159.4 75.8 all-gather.22
  239.1 62.6 all-reduce.14
  304.3 75.8 all-gather.24
  384.1 62.6 all-reduce.16
  449.7 75.8 all-gather.26
  529.5 62.6 all-reduce.18
  594.8 75.8 all-gather.28
  674.6 62.6 all-reduce.20
  740.3 75.8 all-gather.30
  820.2 62.7 all-reduce.22
  885.6 75.8 all-gather.32
  965.3 62.6 all-reduce.24
  1030.9 75.8 all-gather.34
  1110.6 62.6 all-reduce.26
  1175.8 75.8 all-gather.36
  1255.6 62.6 all-reduce.28
  1321.2 75.8 all-gather.38
  1401.0 62.6 all-reduce.30
where the time goes:
time: 1470 us
  waiting for transfers between devices  1390 us (95%)
  matrix products  40.5 us (3%)
  local copies, waits for them, and re-layouts  18.7 us (1%)
    all_gather x10, waiting for transfers between devices, spread(): whole = lax.all_gather(solved[None], 'prow', axis=0, tiled=True)  760 us
    psum x10, waiting for transfers between devices, solve_level(): total = lax.psum(contract(picked, blocks), 'pcol')  628 us
  transfers between devices with their start and end apart: 20, of which 20 were waited for; matrix products, arithmetic and copies ran while one was open for 1% of the time, Pallas kernels for 0%

commit v1 on v0

--- a/solution.py
+++ b/solution.py
@@ -38,7 +38,10 @@
 def spread(solved):
     ncol = lax.axis_size("pcol")
     column = lax.axis_index("pcol")
-    whole = lax.all_gather(solved[None], "prow", axis=0, tiled=True)
+    target = solved[None]
+    side_arr = jnp.stack([target for _ in range(lax.axis_size("prow"))])
+    part_next = lax.all_to_all(side_arr, "prow", 0, 0)
+    whole = jnp.concatenate(part_next, axis=0)
     whole = whole.reshape(whole.shape[0] // ncol, ncol, whole.shape[1], whole.shape[2])
     return lax.dynamic_index_in_dim(whole, column, 1, keepdims=False)
 

time: 1470 us -> 1290 us (0.88)
  waiting for transfers between devices: 1390 us -> 1100 us
  starting transfers between devices: 0.8 us -> 104 us
    all_gather x10 -> x0, waiting for transfers between devices: 760 us -> none  [spread(): whole = lax.all_gather(solved[None], 'prow', axis=0, tiled=True)]
    all_to_all x0 -> x10, waiting for transfers between devices: none -> 452 us  [spread(): part_next = lax.all_to_all(side_arr, 'prow', 0, 0)]
    all_to_all x0 -> x10, starting transfers between devices: none -> 104 us  [spread(): part_next = lax.all_to_all(side_arr, 'prow', 0, 0)]
    psum x10, waiting for transfers between devices: 628 us -> 646 us  [solve_level(): total = lax.psum(contract(picked, blocks), 'pcol')]
where the time goes in v1:
time: 1290 us
  waiting for transfers between devices  1100 us (85%)
  starting transfers between devices  104 us (8%)
  matrix products  34.2 us (3%)
  local copies, waits for them, and re-layouts  32.5 us (3%)
  between operations  14.1 us (1%)
    psum x10, waiting for transfers between devices, solve_level(): total = lax.psum(contract(picked, blocks), 'pcol')  646 us
    all_to_all x10, waiting for transfers between devices, spread(): part_next = lax.all_to_all(side_arr, 'prow', 0, 0)  452 us
    all_to_all x10, starting transfers between devices, spread(): part_next = lax.all_to_all(side_arr, 'prow', 0, 0)  104 us
  transfers between devices with their start and end apart: 20, of which 20 were waited for; matrix products, arithmetic and copies ran while one was open for 1% of the time, Pallas kernels for 0%

profile of v1, /device:TPU:8, one launch (start us, length us, event | category | flops | bytes accessed | tf_op | source)
XLA Modules:
  0.0 1290.4 jit_solution(15998934381836157143)
XLA Ops:
  9.3 11.8 all-to-all-start
  23.1 45.5 %all-to-all-done = bf16[32,1,128,256]{3,2,1,0:T(8,128)(2,1)S(1)} async-done(((bf16[32,1,128,256]{3,2,1,0:T(8,128)(2,1)}), bf16[32,1,128,256]{3,2,1,0:T(8,128)(2,1)S(1)}, u32[]{:S(2)}, u32[]{:S(2)}) %all-to-all-start) | async-done | bytes 2097184 | tf_op jit(solution)/shard_map/all_to_all | solution.py:43
  71.6 64.2 %all-reduce.13.cloned.1.call-done = f32[128,256]{1,0:T(8,128)} async-done(((f32[128,256]{1,0:T(8,128)}), f32[128,256]{1,0:T(8,128)}) %all-reduce.13.cloned.1.call-update) | async-done | bytes 131088 | tf_op jit(solution)/shard_map/psum | solution.py:33
  138.5 10.2 all-to-all-start.1
  149.5 45.2 %all-to-all-done.1 = bf16[32,1,128,256]{3,2,1,0:T(8,128)(2,1)} async-done(((bf16[32,1,128,256]{3,2,1,0:T(8,128)(2,1)}), bf16[32,1,128,256]{3,2,1,0:T(8,128)(2,1)}, u32[]{:S(2)}, u32[]{:S(2)}) %all-to-all-start.1) | async-done | bytes 2097184 | tf_op jit(solution)/shard_map/all_to_all | solution.py:43
  198.5 64.6 %all-reduce.15.cloned.1.call-done = f32[128,256]{1,0:T(8,128)} async-done(((f32[128,256]{1,0:T(8,128)}), f32[128,256]{1,0:T(8,128)}) %all-reduce.15.cloned.1.call-update) | async-done | bytes 131088 | tf_op jit(solution)/shard_map/psum | solution.py:33
  265.8 10.2 all-to-all-start.2
  276.7 45.3 %all-to-all-done.2 = bf16[32,1,128,256]{3,2,1,0:T(8,128)(2,1)} async-done(((bf16[32,1,128,256]{3,2,1,0:T(8,128)(2,1)}), bf16[32,1,128,256]{3,2,1,0:T(8,128)(2,1)}, u32[]{:S(2)}, u32[]{:S(2)}) %all-to-all-start.2) | async-done | bytes 2097184 | tf_op jit(solution)/shard_map/all_to_all | solution.py:43
  325.8 64.6 %all-reduce.17.cloned.1.call-done = f32[128,256]{1,0:T(8,128)} async-done(((f32[128,256]{1,0:T(8,128)}), f32[128,256]{1,0:T(8,128)}) %all-reduce.17.cloned.1.call-update) | async-done | bytes 131088 | tf_op jit(solution)/shard_map/psum | solution.py:33
  393.1 10.2 all-to-all-start.3
  404.0 45.3 %all-to-all-done.3 = bf16[32,1,128,256]{3,2,1,0:T(8,128)(2,1)} async-done(((bf16[32,1,128,256]{3,2,1,0:T(8,128)(2,1)}), bf16[32,1,128,256]{3,2,1,0:T(8,128)(2,1)}, u32[]{:S(2)}, u32[]{:S(2)}) %all-to-all-start.3) | async-done | bytes 2097184 | tf_op jit(solution)/shard_map/all_to_all | solution.py:43
  450.8 2.2 convolution_bitcast_fusion.6
  453.1 64.6 %all-reduce.19.cloned.1.call-done = f32[128,256]{1,0:T(8,128)} async-done(((f32[128,256]{1,0:T(8,128)}), f32[128,256]{1,0:T(8,128)}) %all-reduce.19.cloned.1.call-update) | async-done | bytes 131088 | tf_op jit(solution)/shard_map/psum | solution.py:33
  520.4 10.2 all-to-all-start.4
  531.3 45.2 %all-to-all-done.4 = bf16[32,1,128,256]{3,2,1,0:T(8,128)(2,1)} async-done(((bf16[32,1,128,256]{3,2,1,0:T(8,128)(2,1)}), bf16[32,1,128,256]{3,2,1,0:T(8,128)(2,1)}, u32[]{:S(2)}, u32[]{:S(2)}) %all-to-all-start.4) | async-done | bytes 2097184 | tf_op jit(solution)/shard_map/all_to_all | solution.py:43
  578.9 2.3 convolution_bitcast_fusion.5
  581.2 64.6 %all-reduce.21.cloned.1.call-done = f32[128,256]{1,0:T(8,128)} async-done(((f32[128,256]{1,0:T(8,128)}), f32[128,256]{1,0:T(8,128)}) %all-reduce.21.cloned.1.call-update) | async-done | bytes 131088 | tf_op jit(solution)/shard_map/psum | solution.py:33
  648.6 10.3 all-to-all-start.5
  660.9 44.0 %all-to-all-done.5 = bf16[32,1,128,256]{3,2,1,0:T(8,128)(2,1)S(1)} async-done(((bf16[32,1,128,256]{3,2,1,0:T(8,128)(2,1)}), bf16[32,1,128,256]{3,2,1,0:T(8,128)(2,1)S(1)}, u32[]{:S(2)}, u32[]{:S(2)}) %all-to-all-start.5) | async-done | bytes 2097184 | tf_op jit(solution)/shard_map/all_to_all | solution.py:43
  707.9 64.5 %all-reduce.23.cloned.1.call-done = f32[128,256]{1,0:T(8,128)} async-done(((f32[128,256]{1,0:T(8,128)}), f32[128,256]{1,0:T(8,128)}) %all-reduce.23.cloned.1.call-update) | async-done | bytes 131088 | tf_op jit(solution)/shard_map/psum | solution.py:33
  775.1 10.3 all-to-all-start.6
  786.2 45.2 %all-to-all-done.6 = bf16[32,1,128,256]{3,2,1,0:T(8,128)(2,1)} async-done(((bf16[32,1,128,256]{3,2,1,0:T(8,128)(2,1)}), bf16[32,1,128,256]{3,2,1,0:T(8,128)(2,1)}, u32[]{:S(2)}, u32[]{:S(2)}) %all-to-all-start.6) | async-done | bytes 2097184 | tf_op jit(solution)/shard_map/all_to_all | solution.py:43
  835.2 64.6 %all-reduce.25.cloned.1.call-done = f32[128,256]{1,0:T(8,128)} async-done(((f32[128,256]{1,0:T(8,128)}), f32[128,256]{1,0:T(8,128)}) %all-reduce.25.cloned.1.call-update) | async-done | bytes 131088 | tf_op jit(solution)/shard_map/psum | solution.py:33
  902.5 10.2 all-to-all-start.7
  913.4 45.3 %all-to-all-done.7 = bf16[32,1,128,256]{3,2,1,0:T(8,128)(2,1)} async-done(((bf16[32,1,128,256]{3,2,1,0:T(8,128)(2,1)}), bf16[32,1,128,256]{3,2,1,0:T(8,128)(2,1)}, u32[]{:S(2)}, u32[]{:S(2)}) %all-to-all-start.7) | async-done | bytes 2097184 | tf_op jit(solution)/shard_map/all_to_all | solution.py:43
  962.5 64.6 %all-reduce.27.cloned.1.call-done = f32[128,256]{1,0:T(8,128)} async-done(((f32[128,256]{1,0:T(8,128)}), f32[128,256]{1,0:T(8,128)}) %all-reduce.27.cloned.1.call-update) | async-done | bytes 131088 | tf_op jit(solution)/shard_map/psum | solution.py:33
  1029.8 10.2 all-to-all-start.8
  1040.7 45.3 %all-to-all-done.8 = bf16[32,1,128,256]{3,2,1,0:T(8,128)(2,1)} async-done(((bf16[32,1,128,256]{3,2,1,0:T(8,128)(2,1)}), bf16[32,1,128,256]{3,2,1,0:T(8,128)(2,1)}, u32[]{:S(2)}, u32[]{:S(2)}) %all-to-all-start.8) | async-done | bytes 2097184 | tf_op jit(solution)/shard_map/all_to_all | solution.py:43
  1089.8 64.6 %all-reduce.29.cloned.1.call-done = f32[128,256]{1,0:T(8,128)} async-done(((f32[128,256]{1,0:T(8,128)}), f32[128,256]{1,0:T(8,128)}) %all-reduce.29.cloned.1.call-update) | async-done | bytes 131088 | tf_op jit(solution)/shard_map/psum | solution.py:33
  1157.0 10.2 all-to-all-start.9
  1167.9 45.3 %all-to-all-done.9 = bf16[32,1,128,256]{3,2,1,0:T(8,128)(2,1)} async-done(((bf16[32,1,128,256]{3,2,1,0:T(8,128)(2,1)}), bf16[32,1,128,256]{3,2,1,0:T(8,128)(2,1)}, u32[]{:S(2)}, u32[]{:S(2)}) %all-to-all-start.9) | async-done | bytes 2097184 | tf_op jit(solution)/shard_map/all_to_all | solution.py:43
  1217.0 64.6 %all-reduce.31.cloned.1.call-done = f32[128,256]{1,0:T(8,128)} async-done(((f32[128,256]{1,0:T(8,128)}), f32[128,256]{1,0:T(8,128)}) %all-reduce.31.cloned.1.call-update) | async-done | bytes 131088 | tf_op jit(solution)/shard_map/psum | solution.py:33
  (121 shorter events, 70.6 us)
Async XLA Ops:
  9.3 11.9 copy-start.3
  9.3 13.2 %copy-start.6 = (s32[1,5,6]{2,0,1:T(1,128)S(1)}, s32[1,5,6]{2,0,1:T(1,128)}, u32[]{:S(2)}) copy-start(s32[1,5,6]{2,0,1:T(1,128)} %param.33) | copy-start | bytes 364
  9.3 13.2 %copy-start.7 = (s32[1,5,6]{2,0,1:T(1,128)S(1)}, s32[1,5,6]{2,0,1:T(1,128)}, u32[]{:S(2)}) copy-start(s32[1,5,6]{2,0,1:T(1,128)} %param.36) | copy-start | bytes 364
  9.3 59.3 %all-to-all-start = ((bf16[32,1,128,256]{3,2,1,0:T(8,128)(2,1)}), bf16[32,1,128,256]{3,2,1,0:T(8,128)(2,1)S(1)}, u32[]{:S(2)}, u32[]{:S(2)}) async-start(bf16[32,1,128,256]{3,2,1,0:T(8,128)(2,1)} %stack.51), calls=%async_computation | async-start | bytes 4194304 | tf_op jit(solution)/shard_map/all_to_all | solution.py:43
  21.1 114.7 %all-reduce.13.cloned.1.call-start = ((), (), s32[]{:S(2)}) async-start(), calls=%async_computation.10 | async-start | bytes 262144 | tf_op jit(solution)/shard_map/psum | solution.py:33
  68.6 67.2 %copy-start.1 = (bf16[1,6,256,256]{3,2,1,0:T(8,128)(2,1)S(1)}, bf16[1,6,256,256]{3,2,1,0:T(8,128)(2,1)}, u32[]{:S(2)}) copy-start(bf16[1,6,256,256]{3,2,1,0:T(8,128)(2,1)} %param.30) | copy-start | bytes 2359300
  68.6 67.2 %copy-start.2 = (bf16[1,6,128,256]{3,2,1,0:T(8,128)(2,1)S(1)}, bf16[1,6,128,256]{3,2,1,0:T(8,128)(2,1)}, u32[]{:S(2)}) copy-start(bf16[1,6,128,256]{3,2,1,0:T(8,128)(2,1)} %param.29) | copy-start | bytes 1179652
  138.5 56.2 %all-to-all-start.1 = ((bf16[32,1,128,256]{3,2,1,0:T(8,128)(2,1)}), bf16[32,1,128,256]{3,2,1,0:T(8,128)(2,1)}, u32[]{:S(2)}, u32[]{:S(2)}) async-start(bf16[32,1,128,256]{3,2,1,0:T(8,128)(2,1)} %stack.52), calls=%async_computation.1 | async-start | bytes 4194304 | tf_op jit(solution)/shard_map/all_to_all | solution.py:43
  148.8 114.4 %all-reduce.15.cloned.1.call-start = ((), (), s32[]{:S(2)}) async-start(), calls=%async_computation.11 | async-start | bytes 262144 | tf_op jit(solution)/shard_map/psum | solution.py:33
  265.8 56.2 %all-to-all-start.2 = ((bf16[32,1,128,256]{3,2,1,0:T(8,128)(2,1)}), bf16[32,1,128,256]{3,2,1,0:T(8,128)(2,1)}, u32[]{:S(2)}, u32[]{:S(2)}) async-start(bf16[32,1,128,256]{3,2,1,0:T(8,128)(2,1)} %stack.53), calls=%async_computation.2 | async-start | bytes 4194304 | tf_op jit(solution)/shard_map/all_to_all | solution.py:43
  276.0 114.4 %all-reduce.17.cloned.1.call-start = ((), (), s32[]{:S(2)}) async-start(), calls=%async_computation.12 | async-start | bytes 262144 | tf_op jit(solution)/shard_map/psum | solution.py:33
  393.1 56.2 %all-to-all-start.3 = ((bf16[32,1,128,256]{3,2,1,0:T(8,128)(2,1)}), bf16[32,1,128,256]{3,2,1,0:T(8,128)(2,1)}, u32[]{:S(2)}, u32[]{:S(2)}) async-start(bf16[32,1,128,256]{3,2,1,0:T(8,128)(2,1)} %stack.54), calls=%async_computation.3 | async-start | bytes 4194304 | tf_op jit(solution)/shard_map/all_to_all | solution.py:43
  403.3 114.4 %all-reduce.19.cloned.1.call-start = ((), (), s32[]{:S(2)}) async-start(), calls=%async_computation.13 | async-start | bytes 262144 | tf_op jit(solution)/shard_map/psum | solution.py:33
  520.4 56.2 %all-to-all-start.4 = ((bf16[32,1,128,256]{3,2,1,0:T(8,128)(2,1)}), bf16[32,1,128,256]{3,2,1,0:T(8,128)(2,1)}, u32[]{:S(2)}, u32[]{:S(2)}) async-start(bf16[32,1,128,256]{3,2,1,0:T(8,128)(2,1)} %stack.55), calls=%async_computation.4 | async-start | bytes 4194304 | tf_op jit(solution)/shard_map/all_to_all | solution.py:43
  530.6 115.2 %copy-start = (bf16[1,6,256,256]{3,2,1,0:T(8,128)(2,1)S(1)}, bf16[1,6,256,256]{3,2,1,0:T(8,128)(2,1)}, u32[]{:S(2)}) copy-start(bf16[1,6,256,256]{3,2,1,0:T(8,128)(2,1)} %param.31) | copy-start | bytes 2359300
  530.6 115.2 %all-reduce.21.cloned.1.call-start = ((), (), s32[]{:S(2)}) async-start(), calls=%async_computation.14 | async-start | bytes 262144 | tf_op jit(solution)/shard_map/psum | solution.py:33
  648.6 10.4 copy-start.4
  648.6 12.2 copy-start.9
  648.6 56.2 %all-to-all-start.5 = ((bf16[32,1,128,256]{3,2,1,0:T(8,128)(2,1)}), bf16[32,1,128,256]{3,2,1,0:T(8,128)(2,1)S(1)}, u32[]{:S(2)}, u32[]{:S(2)}) async-start(bf16[32,1,128,256]{3,2,1,0:T(8,128)(2,1)} %stack.56), calls=%async_computation.5 | async-start | bytes 4194304 | tf_op jit(solution)/shard_map/all_to_all | solution.py:43
  658.9 113.5 %all-reduce.23.cloned.1.call-start = ((), (), s32[]{:S(2)}) async-start(), calls=%async_computation.15 | async-start | bytes 262144 | tf_op jit(solution)/shard_map/psum | solution.py:33
  704.9 0.8 copy-start.10
  775.1 11.1 copy-start.8
  775.1 56.3 %all-to-all-start.6 = ((bf16[32,1,128,256]{3,2,1,0:T(8,128)(2,1)}), bf16[32,1,128,256]{3,2,1,0:T(8,128)(2,1)}, u32[]{:S(2)}, u32[]{:S(2)}) async-start(bf16[32,1,128,256]{3,2,1,0:T(8,128)(2,1)} %stack.57), calls=%async_computation.6 | async-start | bytes 4194304 | tf_op jit(solution)/shard_map/all_to_all | solution.py:43
  785.4 114.4 %all-reduce.25.cloned.1.call-start = ((), (), s32[]{:S(2)}) async-start(), calls=%async_computation.16 | async-start | bytes 262144 | tf_op jit(solution)/shard_map/psum | solution.py:33
  902.5 56.2 %all-to-all-start.7 = ((bf16[32,1,128,256]{3,2,1,0:T(8,128)(2,1)}), bf16[32,1,128,256]{3,2,1,0:T(8,128)(2,1)}, u32[]{:S(2)}, u32[]{:S(2)}) async-start(bf16[32,1,128,256]{3,2,1,0:T(8,128)(2,1)} %stack.58), calls=%async_computation.7 | async-start | bytes 4194304 | tf_op jit(solution)/shard_map/all_to_all | solution.py:43
  912.7 114.4 %all-reduce.27.cloned.1.call-start = ((), (), s32[]{:S(2)}) async-start(), calls=%async_computation.17 | async-start | bytes 262144 | tf_op jit(solution)/shard_map/psum | solution.py:33
  1029.8 56.2 %all-to-all-start.8 = ((bf16[32,1,128,256]{3,2,1,0:T(8,128)(2,1)}), bf16[32,1,128,256]{3,2,1,0:T(8,128)(2,1)}, u32[]{:S(2)}, u32[]{:S(2)}) async-start(bf16[32,1,128,256]{3,2,1,0:T(8,128)(2,1)} %stack.59), calls=%async_computation.8 | async-start | bytes 4194304 | tf_op jit(solution)/shard_map/all_to_all | solution.py:43
  1040.0 114.4 %all-reduce.29.cloned.1.call-start = ((), (), s32[]{:S(2)}) async-start(), calls=%async_computation.18 | async-start | bytes 262144 | tf_op jit(solution)/shard_map/psum | solution.py:33
  1157.0 56.2 %all-to-all-start.9 = ((bf16[32,1,128,256]{3,2,1,0:T(8,128)(2,1)}), bf16[32,1,128,256]{3,2,1,0:T(8,128)(2,1)}, u32[]{:S(2)}, u32[]{:S(2)}) async-start(bf16[32,1,128,256]{3,2,1,0:T(8,128)(2,1)} %stack.60), calls=%async_computation.9 | async-start | bytes 4194304 | tf_op jit(solution)/shard_map/all_to_all | solution.py:43
  1167.2 114.3 %all-reduce.31.cloned.1.call-start = ((), (), s32[]{:S(2)}) async-start(), calls=%async_computation.19 | async-start | bytes 262144 | tf_op jit(solution)/shard_map/psum | solution.py:33
  1282.8 0.7 copy-start.5
Sparse Core Ops, SparseCore 0:
  71.7 64.0 all-reduce.12
  198.6 64.4 all-reduce.14
  325.9 64.4 all-reduce.16
  453.2 64.4 all-reduce.18
  581.3 64.4 all-reduce.20
  708.0 64.3 all-reduce.22
  835.3 64.4 all-reduce.24
  962.6 64.4 all-reduce.26
  1089.9 64.4 all-reduce.28
  1217.1 64.4 all-reduce.30
